TPU v7x, 32 devices: a whole 2x2x4 slice. The times are simulated.
32 devices in a mesh: groups: 2 (over y), tiles: 4 (over z), freq: 2 (over x), field: 2 (over core).
Axes of the slice: x: 2, y: 2, z: 4, core: 2. Of those that a mesh axis runs over, the one named last changes fastest.
Arguments:
- fields: bfloat16 [2, 4, 512, 1024], P('field', 'tiles', ('groups', 'freq')), parts along dimension 2, may hold values from -7.5 to 7.5
- slot_tile_ids: int32 [4], replicated, may hold values from 0 to 3, each once
- neighbour_tile_ids: int32 [4, 4], replicated, may hold values from 0 to 3
- neighbour_rotation_code: int32 [4, 4], replicated, may hold values from 0 to 7
- paired_tile_ids: int32 [4, 2], P('tiles'), may hold values from 0 to 3
Outputs:
- csd: float32 [8, 2, 2, 32, 128, 128], P(('groups', 'tiles'), None, None, ('freq', 'field')), parts along dimension 0
There are 2 independent parts, one for each index of `groups`. A program takes and returns all parts, laid end to end along the dimension named above; an argument that names none is the same for every part. Nothing has to cross between parts.
All inputs are finite; a program needn't handle non-finite values.
Results may differ from a plain program's by a relative error of at most 0.0095.
Values may be sent and summed in bfloat16 or wider, within the bound.
A program may use at most 64 MiB of HBM per device.

v0:
```python
import math
import jax
import jax.numpy as jnp
from jax import lax
from jax.sharding import PartitionSpec as P

SIDE = 32
SEGLEN = 64
diffusion = 0.25


def slot_lookup(slot_tile_ids, tile_ids):
    matches = (slot_tile_ids[None, :] == tile_ids.reshape(-1)[:, None]).astype(jnp.int32)
    positions = jnp.sum(
        matches * jnp.arange(slot_tile_ids.shape[0], dtype=jnp.int32)[None, :], axis=1
    )
    return positions.reshape(tile_ids.shape)


def tile_edges(field, tile_side):
    cell_count = field.shape[-1]
    north = field[..., :tile_side]
    east = field[..., tile_side - 1 :: tile_side]
    south = field[..., cell_count - tile_side :]
    west = field[..., ::tile_side]
    return jnp.stack([north, east, south, west], axis=-3)


def inner_edges(field, tile_side):
    cell_count = field.shape[-1]
    north = field[..., tile_side : 2 * tile_side]
    east = field[..., tile_side - 2 :: tile_side]
    south = field[..., cell_count - 2 * tile_side : cell_count - tile_side]
    west = field[..., 1::tile_side]
    return jnp.stack([north, east, south, west], axis=-3)


def pick_rims(all_edges, near_slots, codes):
    chosen = all_edges[near_slots, codes % 4]
    flipped = chosen[..., ::-1]
    return jnp.where((codes // 4 == 1)[:, :, None, None], flipped, chosen)


def smooth_step(field, rims, tile_side):
    cell_count = field.shape[-1]
    values = field.astype(jnp.float32)
    edge_vals = rims.astype(jnp.float32)
    above_row = jnp.concatenate([edge_vals[:, 0], values[..., : cell_count - tile_side]], axis=-1)
    below_row = jnp.concatenate([values[..., tile_side:], edge_vals[:, 2]], axis=-1)
    column_pos = jnp.arange(cell_count, dtype=jnp.int32) % tile_side
    west_full = jnp.repeat(edge_vals[:, 3], tile_side, axis=-1)
    east_full = jnp.repeat(edge_vals[:, 1], tile_side, axis=-1)
    leftward = jnp.where(column_pos == 0, west_full, jnp.roll(values, 1, axis=-1))
    rightward = jnp.where(column_pos == tile_side - 1, east_full, jnp.roll(values, -1, axis=-1))
    laplace = above_row + below_row + leftward + rightward - 4.0 * values
    return (values + diffusion * laplace).astype(jnp.bfloat16)


def before_along(values, first):
    return jnp.concatenate([first[..., None], values[..., :-1]], axis=-1)


def after_along(values, last):
    return jnp.concatenate([values[..., 1:], last[..., None]], axis=-1)


def smooth_one(values, above, below, leftward, rightward):
    laplace = above + below + leftward + rightward - 4.0 * values
    return (values + diffusion * laplace).astype(jnp.bfloat16)


def edge_sweep(outer, inner, rims):
    outer_vals = outer.astype(jnp.float32)
    inner_vals = inner.astype(jnp.float32)
    rim_vals = rims.astype(jnp.float32)
    north_rim = rim_vals[:, 0]
    east_rim = rim_vals[:, 1]
    south_rim = rim_vals[:, 2]
    west_rim = rim_vals[:, 3]
    north = outer_vals[:, 0]
    east = outer_vals[:, 1]
    south = outer_vals[:, 2]
    west = outer_vals[:, 3]
    new_north = smooth_one(
        north,
        north_rim,
        inner_vals[:, 0],
        before_along(north, west_rim[..., 0]),
        after_along(north, east_rim[..., 0]),
    )
    new_east = smooth_one(
        east,
        before_along(east, north_rim[..., -1]),
        after_along(east, south_rim[..., -1]),
        inner_vals[:, 1],
        east_rim,
    )
    new_south = smooth_one(
        south,
        inner_vals[:, 2],
        south_rim,
        before_along(south, west_rim[..., -1]),
        after_along(south, east_rim[..., -1]),
    )
    new_west = smooth_one(
        west,
        before_along(west, north_rim[..., 0]),
        after_along(west, south_rim[..., 0]),
        west_rim,
        inner_vals[:, 3],
    )
    return jnp.stack([new_north, new_east, new_south, new_west], axis=1)


def coarse_sums(field, tile_side):
    leading = field.shape[:-1]
    blocks = field.astype(jnp.float32).reshape(leading + (tile_side // 2, 2, tile_side // 4, 4))
    return jnp.sum(blocks, axis=(-3, -1)).reshape(leading + (tile_side // 2 * (tile_side // 4),))


def window_table(seg_length):
    samples = jnp.arange(seg_length, dtype=jnp.int32)
    frequency = jnp.arange(seg_length // 2, dtype=jnp.int32)
    products = frequency[:, None] * samples[None, :] % seg_length
    angles = 2.0 * math.pi / seg_length * products.astype(jnp.float32)
    window = 0.5 - 0.5 * jnp.cos(2.0 * math.pi / seg_length * samples.astype(jnp.float32))
    dft_table = jnp.stack([window[None, :] * jnp.cos(angles), -window[None, :] * jnp.sin(angles)])
    return (dft_table, jnp.sum(window * window))


def segment_spectra(coarse, dft_table):
    leading = coarse.shape[0]
    segments = coarse.reshape(leading, -1, dft_table.shape[-1], coarse.shape[-1])
    spectra = jnp.einsum("cft,nstp->nscfp", dft_table, segments, precision=lax.Precision.HIGHEST)
    return spectra.astype(jnp.bfloat16)


def cross_density(height, partner, window_power):
    rotated = jnp.stack([height[:, :, 1], -height[:, :, 0]], axis=2)
    stacked = jnp.stack([height, rotated], axis=1)
    cross = jnp.einsum(
        "noscfi,nkscfj->nkofij", stacked, partner, preferred_element_type=jnp.float32
    )
    return cross / (partner.shape[2] * window_power)


def shards(fields, slot_tile_ids, neighbour_tile_ids, neighbour_rotation_code, paired_tile_ids):
    field = fields[0]
    local_count = field.shape[0]
    first_local = lax.axis_index("tiles") * local_count
    near_all = slot_lookup(slot_tile_ids, neighbour_tile_ids)
    near_local = lax.dynamic_slice_in_dim(near_all, first_local, local_count, 0)
    code_local = lax.dynamic_slice_in_dim(neighbour_rotation_code, first_local, local_count, 0)
    every_outer = lax.all_gather(tile_edges(field, SIDE), "tiles", axis=0, tiled=True)
    every_inner = lax.all_gather(inner_edges(field, SIDE), "tiles", axis=0, tiled=True)
    every_rim = pick_rims(every_outer, near_all, neighbour_rotation_code)
    local_rim = lax.dynamic_slice_in_dim(every_rim, first_local, local_count, 0)
    field = smooth_step(field, local_rim, SIDE)
    new_edges = edge_sweep(every_outer, every_inner, every_rim)
    field = smooth_step(field, pick_rims(new_edges, near_local, code_local), SIDE)
    dft_table, window_power = window_table(SEGLEN)
    spectra = segment_spectra(coarse_sums(field, SIDE), dft_table)
    banded = lax.all_to_all(
        lax.all_to_all(spectra[None], "freq", split_axis=4, concat_axis=2, tiled=True),
        "field",
        split_axis=4,
        concat_axis=0,
        tiled=True,
    )
    partner_slots = slot_lookup(slot_tile_ids, paired_tile_ids)
    every_band = lax.all_gather(banded, "tiles", axis=1, tiled=True)
    first_slot = lax.axis_index("tiles") * banded.shape[1]
    height = lax.dynamic_slice_in_dim(every_band[0], first_slot, banded.shape[1], 0)
    velocity = every_band[1]
    return cross_density(height, velocity[partner_slots], window_power)


def solution(mesh):
    placed = (P("field", "tiles", ("groups", "freq"), None), P(), P(), P(), P("tiles", None))
    return jax.shard_map(
        shards,
        mesh=mesh,
        in_specs=placed,
        out_specs=P(("groups", "tiles"), None, None, ("freq", "field"), None, None),
        check_vma=False,
    )
```

profile of v0, /device:TPU:0, one launch (start us, length us, event | category | flops | bytes accessed | tf_op | source)
XLA Modules:
  0.0 69.6 jit_solution(6394495090829797569)
XLA Ops:
  0.1 0.8 %eq.65 = s32[16]{0:T(128)S(1)} reshape(s32[4,4]{1,0:T(4,128)} %param.7) | data formatting | bytes 128 | tf_op jit(solution)/shard_map/eq | solution.py:13
  0.9 0.7 %select_reduce_fusion = s32[16]{0:T(128)S(1)} fusion(s32[16]{0:T(128)S(1)} %eq.65, s32[4]{0:T(128)} %param.6), kind=kLoop, calls=%fused_computation.163 | loop fusion | flops 176 | bytes 144 | tf_op jit(solution)/shard_map/reduce_sum | solution.py:14
  1.6 0.1 reshape.896
  1.7 0.1 reshape.895
  1.8 0.1 broadcast_compare_fusion
  1.9 1.1 %copy.181 = bf16[1,1,128,1024]{2,3,1,0:T(8,128)(2,1)S(1)} copy(bf16[1,1,128,1024]{3,2,1,0:T(8,128)(2,1)} %param.5) | data formatting | bytes 524288 | tf_op args[0]
  3.0 0.1 slice.203
  3.0 0.1 slice.187
  3.1 0.1 slice.201
  3.2 0.1 slice.185
  3.3 0.0 copy-start
  3.3 1.0 %fusion.83 = (f32[1,128,992]{1,2,0:T(8,128)}, f32[1,128,992]{1,2,0:T(8,128)}) fusion(f32[1,128,1024]{1,2,0:T(8,128)S(1)} %bitcast_convert_fusion), kind=kLoop, calls=%fused_computation.197 | loop fusion | bytes 2031616 | tf_op jit(solution)/shard_map/slice | solution.py:48
  4.3 0.1 fusion.81
  4.4 0.0 copy-done
  4.5 0.1 reshape.901
  4.6 15.1 %all_gather.9 = bf16[4,4,128,32]{2,3,1,0:T(8,128)(2,1)S(1)} all-gather(bf16[1,4,128,32]{2,3,1,0:T(8,128)(2,1)S(1)} %pad_maximum_fusion.5), channel_id=1, replica_groups=mesh['groups'=2,'tiles'=4,'freq'=2,'field'=2] {'tiles'}, dimensions={0}, use_global_device_ids=true | all-gather | bytes 163840 | tf_op jit(solution)/shard_map/all_gather | solution.py:154
  19.7 0.6 gather_fusion
  20.3 0.1 rev.6
  20.3 0.1 fusion.77
  20.5 2.2 %fusion.14 = (f32[1,128,1024]{1,2,0:T(8,128)S(1)}, f32[1,128,1024]{1,2,0:T(8,128)S(1)}, f32[1,128,1024]{1,2,0:T(8,128)S(1)}, f32[1,128,1024]{1,2,0:T(8,128)S(1)}) fusion(f32[128,32]{0,1:T(8,128)S(1)} %get-tuple-element.45, f32[128,32]{0,1:T(8,128)S(1)} %get-tuple-element.44, pred[1024]{0:T(1024)(128)(4,1)S(1)} %get-tuple-element.75, ...), kind=kLoop, calls=%fused_computation.32 | loop fusion | flops 2097152 | bytes 4491264 | tf_op jit(solution)/shard_map/convert_element_type | solution.py:46
  22.7 1.0 %fusion.80 = (f32[1,128,992]{1,2,0:T(8,128)}, f32[1,128,992]{1,2,0:T(8,128)}) fusion(f32[1,128,1024]{1,2,0:T(8,128)S(1)} %get-tuple-element.9), kind=kLoop, calls=%fused_computation.194 | loop fusion | bytes 2031616 | tf_op jit(solution)/shard_map/slice | solution.py:49
  23.7 0.1 fusion.79
  23.8 13.5 %all_gather.10 = bf16[4,4,128,32]{2,3,1,0:T(8,128)(2,1)S(1)} all-gather(bf16[1,4,128,32]{2,3,1,0:T(8,128)(2,1)S(1)} %pad_maximum_fusion.6), channel_id=1, replica_groups=mesh['groups'=2,'tiles'=4,'freq'=2,'field'=2] {'tiles'}, dimensions={0}, use_global_device_ids=true | all-gather | bytes 163840 | tf_op jit(solution)/shard_map/all_gather | solution.py:155
  37.5 0.1 fusion.41
  37.6 0.1 fusion.33
  37.7 0.6 gather_fusion.1
  38.3 0.1 fusion.50
  38.5 1.2 %maximum_add_fusion.1 = f32[1,128,1024]{1,2,0:T(8,128)S(1)} fusion(f32[1,128,992]{1,2,0:T(8,128)} %get-tuple-element.22, f32[1,128,32]{1,2,0:T(8,128)S(1)} %get-tuple-element.52, f32[1,128,32]{1,2,0:T(8,128)S(1)} %get-tuple-element.51, f32[1,128,992]{1,2,0:T(8,128)} %get-tuple-element.21), kind=kLoop, calls=%fused_computation.20 | loop fusion | flops 393216 | bytes 1572864 | tf_op jit(solution)/shard_map/add | solution.py:55
  39.8 0.0 copy-start.1
  39.8 0.0 copy-start.2
  39.8 1.3 %convert_reduce_fusion = f32[128,16,8]{0,2,1:T(8,128)S(1)} fusion(f32[1,128,16,2,8,4]{1,5,4,3,2,0:T(4,128)S(1)} %bitcast.265, f32[128,16,2]{0,2,1:T(2,128)S(1)} %bitcast.274, f32[1,128,16,2,8,4]{1,5,4,3,2,0:T(4,128)S(1)} %bitcast.263, f32[1,128,16,2,8,4]{1,5,4,3,2,0:T(4,128)S(1)} %bitcast.264, f32[128,16,2]{0,2,1:T(2,128)S(1)} %bitcast.273, ...), kind=kLoop, calls=%fused_computation.31 | loop fusion | flops 2867200 | bytes 3540992 | tf_op jit(solution)/shard_map/reduce_sum | solution.py:118
  41.1 0.1 reshape.897
  41.2 0.1 sine_multiply_fusion
  41.3 0.3 fusion.1
  41.6 0.6 copy.200
  42.2 3.3 %all-to-all-start = ((bf16[1,1,2,2,32,128]{5,3,2,1,0,4:T(2,128)(2,1)}), bf16[1,1,2,2,32,128]{5,3,2,1,0,4:T(2,128)(2,1)S(1)}, u32[]{:S(2)}, u32[]{:S(2)}) async-start(bf16[1,1,2,2,32,128]{5,3,2,1,0,4:T(2,128)(2,1)} %copy.200), calls=%async_computation | async-start | bytes 65536 | tf_op jit(solution)/shard_map/all_to_all | solution.py:164
  45.5 0.0 copy-done.1
  45.5 0.0 copy-done.2
  45.5 0.2 fusion.70
  45.7 0.7 multiply_reduce_fusion
  47.0 2.4 %all-to-all-done = bf16[1,1,2,2,32,128]{5,3,2,1,0,4:T(2,128)(2,1)S(1)} async-done(((bf16[1,1,2,2,32,128]{5,3,2,1,0,4:T(2,128)(2,1)}), bf16[1,1,2,2,32,128]{5,3,2,1,0,4:T(2,128)(2,1)S(1)}, u32[]{:S(2)}, u32[]{:S(2)}) %all-to-all-start) | async-done | bytes 32800 | tf_op jit(solution)/shard_map/all_to_all | solution.py:164
  49.5 3.7 %all_to_all.36 = bf16[1,1,4,2,16,128]{5,3,2,1,0,4:T(2,128)(2,1)S(1)} all-to-all(bf16[1,1,4,2,16,128]{5,3,2,1,0,4:T(2,128)(2,1)S(1)} %copy.203), channel_id=1, replica_groups=mesh['groups'=2,'tiles'=4,'freq'=2,'field'=2] {'field'}, dimensions={4} | all-to-all | bytes 65536 | tf_op jit(solution)/shard_map/all_to_all | solution.py:163
  53.2 13.4 %all-gather = bf16[2,4,1,4,2,8,128]{6,5,4,3,1,2,0:T(8,128)(2,1)S(1)} all-gather(bf16[2,1,1,4,2,8,128]{6,5,4,3,1,2,0:T(8,128)(2,1)S(1)} %bitcast.267), channel_id=2, replica_groups=mesh['groups'=2,'tiles'=4,'freq'=2,'field'=2] {'tiles'}, dimensions={1}, use_global_device_ids=true | all-gather | bytes 163840 | tf_op jit(solution)/shard_map/all_gather | solution.py:171
  66.7 0.6 gather_fusion.2
  67.3 0.5 fusion
  67.8 1.8 %copy.209 = f32[1,2,2,8,128,128]{5,4,3,2,1,0:T(8,128)} copy(f32[1,2,2,8,128,128]{4,5,2,1,3,0:T(8,128)S(1)} %fusion) | data formatting | bytes 4194304 | tf_op jit(solution)/shard_map/div | solution.py:144
  (43 shorter events, 0.6 us)
Async XLA Ops:
  3.3 1.1 %copy-start = (s32[4,4]{1,0:T(4,128)S(1)}, s32[4,4]{1,0:T(4,128)}, u32[]{:S(2)}) copy-start(s32[4,4]{1,0:T(4,128)} %param.8) | copy-start | bytes 196
  39.8 5.7 %copy-start.1 = (s32[4]{0:T(128)S(1)}, s32[4]{0:T(128)}, u32[]{:S(2)}) copy-start(s32[4]{0:T(128)} %param.6) | copy-start | bytes 52
  39.8 5.7 %copy-start.2 = (s32[1,2]{1,0:T(1,128)S(1)}, s32[1,2]{1,0:T(1,128)}, u32[]{:S(2)}) copy-start(s32[1,2]{1,0:T(1,128)} %param.9) | copy-start | bytes 28
  42.2 7.2 %all-to-all-start = ((bf16[1,1,2,2,32,128]{5,3,2,1,0,4:T(2,128)(2,1)}), bf16[1,1,2,2,32,128]{5,3,2,1,0,4:T(2,128)(2,1)S(1)}, u32[]{:S(2)}, u32[]{:S(2)}) async-start(bf16[1,1,2,2,32,128]{5,3,2,1,0,4:T(2,128)(2,1)} %copy.200), calls=%async_computation | async-start | bytes 65536 | tf_op jit(solution)/shard_map/all_to_all | solution.py:164
where the time goes:
time: 70 us; the launch traced here: 69.6 us
  blocking collectives  45.8 us (65%)
  local copies, waits for them, and re-layouts  9.18 us (13%)
  other arithmetic  7.23 us (10%)
  starting transfers between devices  3.26 us (5%)
  waiting for transfers between devices  2.42 us (3%)
  between operations  1.03 us (1%)
  matrix products  0.77 us (1%)
    all_gather x1, blocking collectives, shards(): lax.all_gather(tile_edges(field, SIDE), 'tiles', axis=0, tiled=True)  15.1 us
    all_gather x1, blocking collectives, shards(): lax.all_gather(inner_edges(field, SIDE), 'tiles', axis=0, tiled=True)  13.5 us
    all_gather x1, blocking collectives, shards(): every_band = lax.all_gather(banded, 'tiles', axis=1, tiled=True)  13.4 us
    all_to_all x1, blocking collectives, shards(): lax.all_to_all(lax.all_to_all(spectra[None], 'freq', split_axis=4, concat...  3.75 us
    all_to_all x1, starting transfers between devices, shards(): lax.all_to_all(spectra[None], 'freq', split_axis=4, concat_axis=2, tiled=...  3.26 us
    all_to_all x1, waiting for transfers between devices, shards(): lax.all_to_all(spectra[None], 'freq', split_axis=4, concat_axis=2, tiled=...  2.42 us
    convert_element_type x2, other arithmetic, smooth_step(): values = field.astype(jnp.float32)  2.21 us
    div x1, local copies, waits for them, and re-layouts, cross_density(): return cross / (partner.shape[2] * window_power)  1.81 us
  transfers between devices with their start and end apart: 1, of which 1 were waited for; matrix products, arithmetic and copies ran while one was open for 1% of the time, Pallas kernels for 0%

commit v1 on v0

--- a/solution.py
+++ b/solution.py
@@ -161,7 +161,12 @@
     dft_table, window_power = window_table(SEGLEN)
     spectra = segment_spectra(coarse_sums(field, SIDE), dft_table)
     banded = lax.all_to_all(
-        lax.all_to_all(spectra[None], "freq", split_axis=4, concat_axis=2, tiled=True),
+        jnp.concatenate(
+            lax.all_to_all(
+                jnp.stack(jnp.split(spectra[None], lax.axis_size("freq"), axis=4)), "freq", 0, 0
+            ),
+            axis=2,
+        ),
         "field",
         split_axis=4,
         concat_axis=0,

time: 70 us -> 70 us (level)
  no operation moved by 1% of the time
where the time goes in v1:
time: 70 us; the launch traced here: 69.6 us
  blocking collectives  45.8 us (65%)
  local copies, waits for them, and re-layouts  8.53 us (12%)
  other arithmetic  7.87 us (11%)
  starting transfers between devices  3.26 us (5%)
  waiting for transfers between devices  2.39 us (3%)
  between operations  1.03 us (1%)
  matrix products  0.77 us (1%)
    all_gather x1, blocking collectives, shards(): lax.all_gather(tile_edges(field, SIDE), 'tiles', axis=0, tiled=True)  15.1 us
    all_gather x1, blocking collectives, shards(): lax.all_gather(inner_edges(field, SIDE), 'tiles', axis=0, tiled=True)  13.5 us
    all_gather x1, blocking collectives, shards(): every_band = lax.all_gather(banded, 'tiles', axis=1, tiled=True)  13.4 us
    all_to_all x1, blocking collectives, shards(): lax.all_to_all(jnp.concatenate(lax.all_to_all(jnp.stack(jnp.split(spectra...  3.75 us
    all_to_all x1, starting transfers between devices, shards(): lax.all_to_all(jnp.stack(jnp.split(spectra[None], lax.axis_size('freq'),...  3.26 us
    all_to_all x1, waiting for transfers between devices, shards(): lax.all_to_all(jnp.stack(jnp.split(spectra[None], lax.axis_size('freq'),...  2.39 us
    convert_element_type x2, other arithmetic, smooth_step(): values = field.astype(jnp.float32)  2.21 us
    div x1, local copies, waits for them, and re-layouts, cross_density(): return cross / (partner.shape[2] * window_power)  1.81 us
  transfers between devices with their start and end apart: 1, of which 1 were waited for; matrix products, arithmetic and copies ran while one was open for 1% of the time, Pallas kernels for 0%

profile of v1, /device:TPU:0, one launch (start us, length us, event | category | flops | bytes accessed | tf_op | source)
XLA Modules:
  0.0 69.6 jit_solution(3412914800968912235)
XLA Ops:
  0.1 0.8 %eq.65 = s32[16]{0:T(128)S(1)} reshape(s32[4,4]{1,0:T(4,128)} %param.7) | data formatting | bytes 128 | tf_op jit(solution)/shard_map/eq | solution.py:13
  0.9 0.7 %select_reduce_fusion = s32[16]{0:T(128)S(1)} fusion(s32[16]{0:T(128)S(1)} %eq.65, s32[4]{0:T(128)} %param.6), kind=kLoop, calls=%fused_computation.166 | loop fusion | flops 176 | bytes 144 | tf_op jit(solution)/shard_map/reduce_sum | solution.py:14
  1.6 0.1 reshape.899
  1.7 0.1 reshape.898
  1.8 0.1 broadcast_compare_fusion
  1.9 1.1 %copy.147 = bf16[1,1,128,1024]{2,3,1,0:T(8,128)(2,1)S(1)} copy(bf16[1,1,128,1024]{3,2,1,0:T(8,128)(2,1)} %param.5) | data formatting | bytes 524288 | tf_op args[0]
  3.0 0.1 slice.203
  3.0 0.1 slice.187
  3.1 0.1 slice.201
  3.2 0.1 slice.185
  3.3 0.0 copy-start
  3.3 1.0 %fusion.83 = (f32[1,128,992]{1,2,0:T(8,128)}, f32[1,128,992]{1,2,0:T(8,128)}) fusion(f32[1,128,1024]{1,2,0:T(8,128)S(1)} %bitcast_convert_fusion), kind=kLoop, calls=%fused_computation.200 | loop fusion | bytes 2031616 | tf_op jit(solution)/shard_map/slice | solution.py:48
  4.3 0.1 fusion.81
  4.4 0.0 copy-done
  4.5 0.1 reshape.905
  4.6 15.1 %all_gather.9 = bf16[4,4,128,32]{2,3,1,0:T(8,128)(2,1)S(1)} all-gather(bf16[1,4,128,32]{2,3,1,0:T(8,128)(2,1)S(1)} %pad_maximum_fusion.5), channel_id=1, replica_groups=mesh['groups'=2,'tiles'=4,'freq'=2,'field'=2] {'tiles'}, dimensions={0}, use_global_device_ids=true | all-gather | bytes 163840 | tf_op jit(solution)/shard_map/all_gather | solution.py:154
  19.7 0.6 gather_fusion
  20.3 0.1 rev.6
  20.3 0.1 fusion.77
  20.5 2.2 %fusion.14 = (f32[1,128,1024]{1,2,0:T(8,128)S(1)}, f32[1,128,1024]{1,2,0:T(8,128)S(1)}, f32[1,128,1024]{1,2,0:T(8,128)S(1)}, f32[1,128,1024]{1,2,0:T(8,128)S(1)}) fusion(f32[128,32]{0,1:T(8,128)S(1)} %get-tuple-element.45, f32[128,32]{0,1:T(8,128)S(1)} %get-tuple-element.44, pred[1024]{0:T(1024)(128)(4,1)S(1)} %get-tuple-element.77, ...), kind=kLoop, calls=%fused_computation.32 | loop fusion | flops 2097152 | bytes 4491264 | tf_op jit(solution)/shard_map/convert_element_type | solution.py:46
  22.7 1.0 %fusion.80 = (f32[1,128,992]{1,2,0:T(8,128)}, f32[1,128,992]{1,2,0:T(8,128)}) fusion(f32[1,128,1024]{1,2,0:T(8,128)S(1)} %get-tuple-element.9), kind=kLoop, calls=%fused_computation.197 | loop fusion | bytes 2031616 | tf_op jit(solution)/shard_map/slice | solution.py:49
  23.7 0.1 fusion.79
  23.8 13.5 %all_gather.10 = bf16[4,4,128,32]{2,3,1,0:T(8,128)(2,1)S(1)} all-gather(bf16[1,4,128,32]{2,3,1,0:T(8,128)(2,1)S(1)} %pad_maximum_fusion.6), channel_id=1, replica_groups=mesh['groups'=2,'tiles'=4,'freq'=2,'field'=2] {'tiles'}, dimensions={0}, use_global_device_ids=true | all-gather | bytes 163840 | tf_op jit(solution)/shard_map/all_gather | solution.py:155
  37.5 0.1 fusion.41
  37.6 0.1 fusion.33
  37.7 0.6 gather_fusion.1
  38.3 0.1 fusion.50
  38.5 1.2 %maximum_add_fusion.1 = f32[1,128,1024]{1,2,0:T(8,128)S(1)} fusion(f32[1,128,992]{1,2,0:T(8,128)} %get-tuple-element.22, f32[1,128,32]{1,2,0:T(8,128)S(1)} %get-tuple-element.52, f32[1,128,32]{1,2,0:T(8,128)S(1)} %get-tuple-element.51, f32[1,128,992]{1,2,0:T(8,128)} %get-tuple-element.21), kind=kLoop, calls=%fused_computation.20 | loop fusion | flops 393216 | bytes 1572864 | tf_op jit(solution)/shard_map/add | solution.py:55
  39.8 0.0 copy-start.1
  39.8 0.0 copy-start.2
  39.8 1.3 %convert_reduce_fusion = f32[128,16,8]{0,2,1:T(8,128)S(1)} fusion(f32[1,128,16,2,8,4]{1,5,4,3,2,0:T(4,128)S(1)} %bitcast.266, f32[128,16,2]{0,2,1:T(2,128)S(1)} %bitcast.274, f32[1,128,16,2,8,4]{1,5,4,3,2,0:T(4,128)S(1)} %bitcast.264, f32[1,128,16,2,8,4]{1,5,4,3,2,0:T(4,128)S(1)} %bitcast.265, f32[128,16,2]{0,2,1:T(2,128)S(1)} %bitcast.273, ...), kind=kLoop, calls=%fused_computation.31 | loop fusion | flops 2867200 | bytes 3540992 | tf_op jit(solution)/shard_map/reduce_sum | solution.py:118
  41.1 0.1 reshape.900
  41.2 0.1 sine_multiply_fusion
  41.3 0.3 fusion.1
  41.6 0.6 pad_maximum_fusion.7
  42.2 3.3 %all-to-all-start = ((bf16[2,1,1,2,2,16,128]{6,5,4,3,2,1,0:T(8,128)(2,1)}), bf16[2,1,1,2,2,16,128]{6,5,4,3,2,1,0:T(8,128)(2,1)S(1)}, u32[]{:S(2)}, u32[]{:S(2)}) async-start(bf16[2,1,1,2,2,16,128]{6,5,4,3,2,1,0:T(8,128)(2,1)} %pad_maximum_fusion.7), calls=%async_computation | async-start | bytes 65536 | tf_op jit(solution)/shard_map/all_to_all | solution.py:165
  45.5 0.0 copy-done.1
  45.5 0.0 copy-done.2
  45.5 0.2 fusion.70
  45.7 0.7 multiply_reduce_fusion
  47.0 2.4 %all-to-all-done = bf16[2,1,1,2,2,16,128]{6,5,4,3,2,1,0:T(8,128)(2,1)S(1)} async-done(((bf16[2,1,1,2,2,16,128]{6,5,4,3,2,1,0:T(8,128)(2,1)}), bf16[2,1,1,2,2,16,128]{6,5,4,3,2,1,0:T(8,128)(2,1)S(1)}, u32[]{:S(2)}, u32[]{:S(2)}) %all-to-all-start) | async-done | bytes 32800 | tf_op jit(solution)/shard_map/all_to_all | solution.py:165
  49.5 3.7 %all_to_all.23 = bf16[1,1,4,2,16,128]{5,3,2,1,0,4:T(2,128)(2,1)S(1)} all-to-all(bf16[1,1,4,2,16,128]{5,3,2,1,0,4:T(2,128)(2,1)S(1)} %copy.166), channel_id=1, replica_groups=mesh['groups'=2,'tiles'=4,'freq'=2,'field'=2] {'field'}, dimensions={4} | all-to-all | bytes 65536 | tf_op jit(solution)/shard_map/all_to_all | solution.py:163
  53.2 13.4 %all-gather = bf16[2,4,1,4,2,8,128]{6,5,4,3,1,2,0:T(8,128)(2,1)S(1)} all-gather(bf16[2,1,1,4,2,8,128]{6,5,4,3,1,2,0:T(8,128)(2,1)S(1)} %bitcast.268), channel_id=2, replica_groups=mesh['groups'=2,'tiles'=4,'freq'=2,'field'=2] {'tiles'}, dimensions={1}, use_global_device_ids=true | all-gather | bytes 163840 | tf_op jit(solution)/shard_map/all_gather | solution.py:176
  66.7 0.6 gather_fusion.2
  67.3 0.5 fusion
  67.8 1.8 %copy.172 = f32[1,2,2,8,128,128]{5,4,3,2,1,0:T(8,128)} copy(f32[1,2,2,8,128,128]{4,5,2,1,3,0:T(8,128)S(1)} %fusion) | data formatting | bytes 4194304 | tf_op jit(solution)/shard_map/div | solution.py:144
  (42 shorter events, 0.6 us)
Async XLA Ops:
  3.3 1.1 %copy-start = (s32[4,4]{1,0:T(4,128)S(1)}, s32[4,4]{1,0:T(4,128)}, u32[]{:S(2)}) copy-start(s32[4,4]{1,0:T(4,128)} %param.8) | copy-start | bytes 196
  39.8 5.7 %copy-start.1 = (s32[4]{0:T(128)S(1)}, s32[4]{0:T(128)}, u32[]{:S(2)}) copy-start(s32[4]{0:T(128)} %param.6) | copy-start | bytes 52
  39.8 5.7 %copy-start.2 = (s32[1,2]{1,0:T(1,128)S(1)}, s32[1,2]{1,0:T(1,128)}, u32[]{:S(2)}) copy-start(s32[1,2]{1,0:T(1,128)} %param.9) | copy-start | bytes 28
  42.2 7.2 %all-to-all-start = ((bf16[2,1,1,2,2,16,128]{6,5,4,3,2,1,0:T(8,128)(2,1)}), bf16[2,1,1,2,2,16,128]{6,5,4,3,2,1,0:T(8,128)(2,1)S(1)}, u32[]{:S(2)}, u32[]{:S(2)}) async-start(bf16[2,1,1,2,2,16,128]{6,5,4,3,2,1,0:T(8,128)(2,1)} %pad_maximum_fusion.7), calls=%async_computation | async-start | bytes 65536 | tf_op jit(solution)/shard_map/all_to_all | solution.py:165
